TPU v7x, 256 devices: a whole 4x4x8 slice. The times are simulated.
256 devices in a mesh: probe: 64 (over z, x_lo, y), slab: 4 (over x_hi, core).
Axes of the slice: x: 4 (x_hi: 2, x_lo: 2; x = x_hi * 2 + x_lo), y: 4, z: 8, core: 2. Of those that a mesh axis runs over, the one named last changes fastest.
Arguments:
- smatrix: bfloat16 [2, 512, 128, 128], P(None, 'probe', 'slab'), may hold values from -6 to 6
- amplitude: float32 [2, 512], replicated, may hold values from -0.25 to 0.25
- beam_index: int32 [512, 2], replicated, may hold values from -32 to 31
- positions: int32 [8192, 2], P('probe'), may hold values from -8 to 8
Outputs:
- patterns: float32 [8192, 128, 128], P('probe', 'slab')
Inputs may be any that keep to these rules, and one draw needn't show every extreme that they name: `positions`: column 0 is the row offset that places a probe's crop in the band, column 1 the column offset. `beam_index`: column 0 along rows, column 1 along columns.
All inputs are finite; a program needn't handle non-finite values.
Results may differ from a plain program's by a relative error of at most 0.0029.
Values may be sent and summed in bfloat16 or wider, within the bound.
A program may use at most 128 MiB of HBM per device.

v0:
```python
import math
import jax
import jax.numpy as jnp
from jax import lax
from jax.sharding import PartitionSpec as P

HALO = 8
SIDE = 2 * HALO + 1
SPOTS = SIDE * SIDE


def dft_table(first, second, length):
    angle = (
        2.0
        * math.pi
        * (jnp.mod(first[:, None] * second[None, :], length).astype(jnp.float32) / length)
    )
    return (jnp.cos(angle), jnp.sin(angle))


def spot_weights(amplitude, beam_index, rows_all, cols):
    spot = jnp.arange(SPOTS, dtype=jnp.int32)
    row, col = (spot // SIDE - HALO, spot % SIDE - HALO)
    turn = jnp.mod(beam_index[:, 0:1] * row[None, :], rows_all).astype(jnp.float32) / rows_all
    turn = turn + jnp.mod(beam_index[:, 1:2] * col[None, :], cols).astype(jnp.float32) / cols
    cosine, sine = (jnp.cos(2.0 * math.pi * turn), jnp.sin(2.0 * math.pi * turn))
    re, im = (amplitude[0][:, None], amplitude[1][:, None])
    return (
        (re * cosine + im * sine).astype(jnp.bfloat16),
        (im * cosine - re * sine).astype(jnp.bfloat16),
    )


def on_device(smatrix, amplitude, beam_index, positions):
    _, beams_here, slab_rows, cols = smatrix.shape
    groups = lax.axis_size("probe")
    slabs = lax.axis_size("slab")
    rows_all = slab_rows * slabs
    own = cols // groups
    highest = lax.Precision.HIGHEST
    f32 = jnp.float32
    index = jnp.arange(cols, dtype=jnp.int32)
    cos, sin = dft_table(index, index, cols)
    cos, sin = (cos / math.sqrt(cols), sin / math.sqrt(cols))
    s_re, s_im = (smatrix[0].astype(f32), smatrix[1].astype(f32))
    mm = lambda a, b: jnp.einsum("lc,brc->lbr", a, b, precision=highest)
    half = jnp.stack([mm(cos, s_re) + mm(sin, s_im), mm(cos, s_im) - mm(sin, s_re)], 1)
    half = half.astype(jnp.bfloat16).reshape(groups, own, 2, beams_here, slab_rows)
    got = lax.all_to_all(half, "probe", split_axis=0, concat_axis=0, tiled=True)
    got = lax.all_gather(got, "slab", axis=0)
    got = jnp.transpose(got, (2, 0, 5, 3, 1, 4)).reshape(own, rows_all, 2, groups * beams_here)
    w_re, w_im = spot_weights(amplitude, beam_index, rows_all, cols)
    field = jnp.concatenate([got[:, :, 0], got[:, :, 1]], axis=-1)
    u_re = jnp.dot(field, jnp.concatenate([w_re, -w_im], 0), preferred_element_type=f32)
    u_im = jnp.dot(field, jnp.concatenate([w_im, w_re], 0), preferred_element_type=f32)
    row = jnp.arange(rows_all, dtype=jnp.int32)[:, None]
    shift = (jnp.arange(SPOTS, dtype=jnp.int32) // SIDE - HALO)[None, :]
    inside = (row >= shift) & (row < rows_all + shift)
    u_re = jnp.where(inside[None], u_re, 0.0)
    u_im = jnp.where(inside[None], u_im, 0.0)
    freq = lax.axis_index("slab") * slab_rows + jnp.arange(slab_rows, dtype=jnp.int32)
    rcos, rsin = dft_table(freq, row[:, 0], rows_all)
    rcos, rsin = (rcos / math.sqrt(rows_all), rsin / math.sqrt(rows_all))
    mm = lambda a, b: jnp.einsum("kr,lrs->lks", a, b, precision=highest)
    out_re = mm(rcos, u_re) + mm(rsin, u_im)
    out_im = mm(rcos, u_im) - mm(rsin, u_re)
    power = (out_re**2 + out_im**2).astype(jnp.bfloat16)
    table = lax.all_gather(power, "probe", axis=0, tiled=True)
    spot = (positions[:, 0] + HALO) * SIDE + positions[:, 1] + HALO
    pick = (spot[:, None] == jnp.arange(SPOTS, dtype=jnp.int32)[None, :]).astype(jnp.bfloat16)
    return jnp.einsum("ps,lks->pkl", pick, table, preferred_element_type=f32)


def solution(mesh):
    return jax.shard_map(
        on_device,
        mesh=mesh,
        in_specs=(P(None, "probe", "slab", None), P(), P(), P("probe", None)),
        out_specs=P("probe", "slab", None),
        check_vma=False,
    )
```

profile of v0, /device:TPU:4, one launch (start us, length us, event | category | flops | bytes accessed | tf_op | source)
XLA Modules:
  0.0 372.4 jit_solution(1641833828458793947)
XLA Ops:
  6.5 0.0 copy-start
  6.5 0.0 copy-start.1
  6.5 1.3 fusion.31
  7.9 1.3 fusion.37
  9.2 1.3 fusion.6
  10.5 1.3 fusion.5
  11.9 0.2 copy.21
  12.1 0.2 copy.22
  12.2 0.1 copy_bitcast_fusion.1
  12.4 1.1 reshape.91
  13.4 12.7 %all-to-all-start = ((bf16[64,2,512]{2,1,0:T(2,128)(2,1)}), bf16[64,2,512]{2,1,0:T(2,128)(2,1)S(1)}, u32[]{:S(2)}, u32[]{:S(2)}) async-start(bf16[64,2,512]{2,1,0:T(2,128)(2,1)} %reshape.91), calls=%async_computation | async-start | bytes 262144 | tf_op jit(solution)/shard_map/all_to_all | solution.py:49
  26.2 0.0 all-gather.3.cloned.1.call-start
  26.3 0.0 copy-done
  26.3 0.0 copy-done.1
  26.3 0.1 fusion.24
  26.5 3.6 fusion.126
  30.1 2.9 subtract_convert_fusion
  33.0 4.1 %all-to-all-done = bf16[64,2,512]{2,1,0:T(2,128)(2,1)S(1)} async-done(((bf16[64,2,512]{2,1,0:T(2,128)(2,1)}), bf16[64,2,512]{2,1,0:T(2,128)(2,1)S(1)}, u32[]{:S(2)}, u32[]{:S(2)}) %all-to-all-start) | async-done | bytes 131104 | tf_op jit(solution)/shard_map/all_to_all | solution.py:49
  37.1 0.3 reshape.92
  37.4 0.1 copy.24
  37.5 15.7 %all-gather = bf16[256,2,2,8,32]{4,3,2,1,0:T(8,128)(2,1)S(1)} all-gather(bf16[64,2,2,8,32]{4,3,2,1,0:T(8,128)(2,1)S(1)} %copy.24), channel_id=2, replica_groups=mesh['probe'=64,'slab'=4] {'slab'}, dimensions={0}, use_global_device_ids=true | all-gather | bytes 655360 | tf_op jit(solution)/shard_map/all_gather | solution.py:50
  53.2 2.7 copy.38
  55.9 1.1 reshape.82
  56.9 0.0 copy-start.3
  57.0 0.1 copy.30
  57.1 0.1 copy.31
  57.3 0.4 convolution_select_fusion
  57.7 0.2 copy-done.3
  57.9 0.0 copy-start.2
  57.9 0.4 convolution_select_fusion.1
  58.3 0.6 fusion.63
  58.9 0.6 fusion.61
  59.5 0.6 fusion.9
  60.1 1.2 fusion.11
  61.3 0.0 all-gather.3.cloned.1.call-update
  61.3 0.0 copy-done.2
  61.4 298.6 %all-gather.3.cloned.1.call-done = bf16[128,32,289]{2,1,0:T(8,128)(2,1)} async-done(((bf16[2,32,289]{2,1,0:T(8,128)(2,1)}), bf16[128,32,289]{2,1,0:T(8,128)(2,1)}) %all-gather.3.cloned.1.call-update) | async-done | bytes 2367504 | tf_op jit(solution)/shard_map/all_gather | solution.py:68
  359.9 3.6 fusion.2
  363.6 2.0 copy.29
  (7 shorter events, 0.1 us)
Async XLA Ops:
  6.5 19.8 %copy-start = (f32[2,512]{1,0:T(2,128)S(1)}, f32[2,512]{1,0:T(2,128)}, u32[]{:S(2)}) copy-start(f32[2,512]{1,0:T(2,128)} %param.5) | copy-start | bytes 12292
  6.5 19.8 %copy-start.1 = (s32[512,2]{0,1:T(2,128)S(1)}, s32[512,2]{0,1:T(2,128)}, u32[]{:S(2)}) copy-start(s32[512,2]{0,1:T(2,128)} %param.6) | copy-start | bytes 12292
  13.4 23.7 %all-to-all-start = ((bf16[64,2,512]{2,1,0:T(2,128)(2,1)}), bf16[64,2,512]{2,1,0:T(2,128)(2,1)S(1)}, u32[]{:S(2)}, u32[]{:S(2)}) async-start(bf16[64,2,512]{2,1,0:T(2,128)(2,1)} %reshape.91), calls=%async_computation | async-start | bytes 262144 | tf_op jit(solution)/shard_map/all_to_all | solution.py:49
  26.2 333.8 %all-gather.3.cloned.1.call-start = ((), (), s32[]{:S(2)}) async-start(), calls=%async_computation.1 | async-start | bytes 3194880 | tf_op jit(solution)/shard_map/all_gather | solution.py:68
  56.9 1.0 copy-start.3
  57.9 3.5 copy-start.2
Sparse Core Ops, SparseCore 0:
  61.5 298.4 all-gather.2
where the time goes:
time: 373 us; the launch traced here: 372 us
  waiting for transfers between devices  303 us (81%)
  blocking collectives  15.7 us (4%)
  between operations  13.6 us (4%)
  starting transfers between devices  12.8 us (3%)
  matrix products  12.7 us (3%)
  local copies, waits for them, and re-layouts  8.13 us (2%)
  other arithmetic  6.82 us (2%)
    all_gather x1, waiting for transfers between devices, on_device(): table = lax.all_gather(power, 'probe', axis=0, tiled=True)  299 us
    all_gather x1, blocking collectives, on_device(): got = lax.all_gather(got, 'slab', axis=0)  15.7 us
    all_to_all x1, starting transfers between devices, on_device(): got = lax.all_to_all(half, 'probe', split_axis=0, concat_axis=0, tiled=True)  12.7 us
  transfers between devices with their start and end apart: 2, of which 2 were waited for; matrix products, arithmetic and copies ran while one was open for 2% of the time, Pallas kernels for 0%

commit v1 on v0

--- a/solution.py
+++ b/solution.py
@@ -65,7 +65,16 @@
     out_re = mm(rcos, u_re) + mm(rsin, u_im)
     out_im = mm(rcos, u_im) - mm(rsin, u_re)
     power = (out_re**2 + out_im**2).astype(jnp.bfloat16)
-    table = lax.all_gather(power, "probe", axis=0, tiled=True)
+    _cut_heaps = lambda row_data: jnp.concatenate(
+        jax.lax.all_to_all(
+            jnp.stack([row_data for _ in range(jax.lax.psum(1, "probe"))]),
+            "probe",
+            split_axis=0,
+            concat_axis=0,
+        ),
+        0,
+    )
+    table = _cut_heaps(power)
     spot = (positions[:, 0] + HALO) * SIDE + positions[:, 1] + HALO
     pick = (spot[:, None] == jnp.arange(SPOTS, dtype=jnp.int32)[None, :]).astype(jnp.bfloat16)
     return jnp.einsum("ps,lks->pkl", pick, table, preferred_element_type=f32)

time: 373 us -> 145 us (0.39)
  waiting for transfers between devices: 303 us -> 77.5 us
  between operations: 13.6 us -> 0.26 us
  starting transfers between devices: 12.8 us -> 20.7 us
    all_gather x1 -> x0, waiting for transfers between devices: 299 us -> none  [on_device(): table = lax.all_gather(power, 'probe', axis=0, tiled=True)]
    all_to_all x0 -> x1, waiting for transfers between devices: none -> 73.4 us  [on_device(): jax.lax.all_to_all(jnp.stack([row_data for _ in range(jax.lax.psum(1, 'pr...]
    all_to_all x0 -> x1, starting transfers between devices: none -> 8 us  [on_device(): jax.lax.all_to_all(jnp.stack([row_data for _ in range(jax.lax.psum(1, 'pr...]
  transfers between devices with their start and end apart: 2 -> 2, of which waited for: 2 -> 2; matrix products, arithmetic and copies ran while one was open for 2% -> 5% of each run, Pallas kernels for 0% -> 0%
where the time goes in v1:
time: 145 us; the launch traced here: 144 us
  waiting for transfers between devices  77.5 us (53%)
  starting transfers between devices  20.7 us (14%)
  blocking collectives  15.7 us (11%)
  local copies, waits for them, and re-layouts  11.7 us (8%)
  matrix products  11.5 us (8%)
  other arithmetic  6.82 us (5%)
    all_to_all x1, waiting for transfers between devices, on_device(): jax.lax.all_to_all(jnp.stack([row_data for _ in range(jax.lax.psum(1, 'pr...  73.4 us
    all_gather x1, blocking collectives, on_device(): got = lax.all_gather(got, 'slab', axis=0)  15.7 us
    all_to_all x1, starting transfers between devices, on_device(): got = lax.all_to_all(half, 'probe', split_axis=0, concat_axis=0, tiled=True)  12.7 us
    all_to_all x1, starting transfers between devices, on_device(): jax.lax.all_to_all(jnp.stack([row_data for _ in range(jax.lax.psum(1, 'pr...  8 us
    dot_general x4, matrix products, on_device(): mm = lambda a, b: jnp.einsum('lc,brc->lbr', a, b, precision=highest)  5.29 us
    all_to_all x1, waiting for transfers between devices, on_device(): got = lax.all_to_all(half, 'probe', split_axis=0, concat_axis=0, tiled=True)  4.12 us
    neg x1, other arithmetic, on_device(): -w_im  3.6 us
    dot_general x1, matrix products, on_device(): return jnp.einsum('ps,lks->pkl', pick, table, preferred_element_type=f32)  3.1 us
  transfers between devices with their start and end apart: 2, of which 2 were waited for; matrix products, arithmetic and copies ran while one was open for 5% of the time, Pallas kernels for 0%

profile of v1, /device:TPU:4, one launch (start us, length us, event | category | flops | bytes accessed | tf_op | source)
XLA Modules:
  0.0 144.3 jit_solution(3149367713366920787)
XLA Ops:
  0.0 0.0 copy-start
  0.0 0.0 copy-start.1
  0.0 1.3 fusion.37
  1.3 1.3 fusion.31
  2.7 1.3 fusion.5
  4.0 0.2 copy.23
  4.2 1.3 fusion.6
  5.5 0.2 copy.24
  5.7 0.1 copy_bitcast_fusion.1
  5.8 1.1 reshape.97
  6.9 12.7 %all-to-all-start = ((bf16[64,2,512]{2,1,0:T(2,128)(2,1)}), bf16[64,2,512]{2,1,0:T(2,128)(2,1)S(1)}, u32[]{:S(2)}, u32[]{:S(2)}) async-start(bf16[64,2,512]{2,1,0:T(2,128)(2,1)} %reshape.97), calls=%async_computation | async-start | bytes 262144 | tf_op jit(solution)/shard_map/all_to_all | solution.py:49
  19.7 0.0 copy-done
  19.7 0.0 copy-done.1
  19.7 0.1 fusion.24
  19.9 3.6 %fusion.126 = bf16[512,289]{0,1:T(8,128)(2,1)} fusion(f32[512]{0:T(512)S(1)} %bitcast.79, s32[289]{0:T(512)S(1)} %get-tuple-element.13, s32[512]{0:T(512)S(1)} %bitcast.83, s32[289]{0:T(512)S(1)} %get-tuple-element.14, s32[512]{0:T(512)S(1)} %bitcast.81, f32[512]{0:T(512)S(1)} %bitcast.77), kind=kLoop, calls=%fused_computation.159 | loop fusion | flops 5178880 | bytes 306440 | tf_op jit(solution)/shard_map/neg | solution.py:54
  23.5 2.9 %subtract_convert_fusion = (bf16[512,289]{0,1:T(8,128)(2,1)S(1)}, bf16[512,289]{0,1:T(8,128)(2,1)S(1)}) fusion(f32[512]{0:T(512)S(1)} %bitcast.78, s32[289]{0:T(512)S(1)} %get-tuple-element.13, s32[512]{0:T(512)S(1)} %bitcast.84, s32[289]{0:T(512)S(1)} %get-tuple-element.14, s32[512]{0:T(512)S(1)} %bitcast.82, f32[512]{0:T(512)S(1)} %bitcast.80), kind=kLoop, calls=%fused_computation.39 | loop fusion | flops 5326848 | bytes 602376 | tf_op jit(solution)/shard_map/convert_element_type | solution.py:30
  26.4 4.1 %all-to-all-done = bf16[64,2,512]{2,1,0:T(2,128)(2,1)S(1)} async-done(((bf16[64,2,512]{2,1,0:T(2,128)(2,1)}), bf16[64,2,512]{2,1,0:T(2,128)(2,1)S(1)}, u32[]{:S(2)}, u32[]{:S(2)}) %all-to-all-start) | async-done | bytes 131104 | tf_op jit(solution)/shard_map/all_to_all | solution.py:49
  30.6 0.3 reshape.98
  30.8 0.1 copy.26
  30.9 15.7 %all-gather = bf16[256,2,2,8,32]{4,3,2,1,0:T(8,128)(2,1)S(1)} all-gather(bf16[64,2,2,8,32]{4,3,2,1,0:T(8,128)(2,1)S(1)} %copy.26), channel_id=2, replica_groups=mesh['probe'=64,'slab'=4] {'slab'}, dimensions={0}, use_global_device_ids=true | all-gather | bytes 655360 | tf_op jit(solution)/shard_map/all_gather | solution.py:50
  46.6 2.7 %copy.40 = bf16[4,64,2,2,8,32]{5,0,4,1,3,2:T(4,128)(2,1)S(1)} copy(bf16[4,64,2,2,8,32]{5,4,3,2,1,0:T(8,128)(2,1)S(1)} %bitcast.68) | data formatting | bytes 1048576 | tf_op jit(solution)/shard_map/all_gather | solution.py:50
  49.3 1.1 reshape.87
  50.4 0.0 copy-start.3
  50.4 0.1 copy.32
  50.6 0.1 copy.33
  50.7 0.6 copy-done.3
  51.3 0.4 convolution_select_fusion.1
  51.7 0.4 convolution_select_fusion
  52.1 0.6 fusion.63
  52.7 0.6 fusion.61
  53.3 0.6 fusion.9
  53.9 0.6 fusion.11
  54.5 2.1 %stack.11 = bf16[64,2,32,289]{3,2,1,0:T(8,128)(2,1)} broadcast(bf16[2,32,289]{2,1,0:T(8,128)(2,1)S(1)} %fusion.11), dimensions={1,2,3} | broadcast | bytes 2404480 | tf_op jit(solution)/shard_map/stack | solution.py:70
  56.7 0.0 copy-start.2
  56.7 8.0 %all-to-all-start.1 = ((bf16[64,2,32,289]{3,2,1,0:T(8,128)(2,1)}), bf16[64,2,32,289]{3,2,1,0:T(8,128)(2,1)S(1)}, u32[]{:S(2)}, u32[]{:S(2)}) async-start(bf16[64,2,32,289]{3,2,1,0:T(8,128)(2,1)} %stack.11), calls=%async_computation.1 | async-start | bytes 6291456 | tf_op jit(solution)/shard_map/all_to_all | solution.py:69
  64.7 0.0 copy-done.2
  64.7 73.4 %all-to-all-done.1 = bf16[64,2,32,289]{3,2,1,0:T(8,128)(2,1)S(1)} async-done(((bf16[64,2,32,289]{3,2,1,0:T(8,128)(2,1)}), bf16[64,2,32,289]{3,2,1,0:T(8,128)(2,1)S(1)}, u32[]{:S(2)}, u32[]{:S(2)}) %all-to-all-start.1) | async-done | bytes 2367520 | tf_op jit(solution)/shard_map/all_to_all | solution.py:69
  138.1 3.1 %fusion.2 = f32[128,32,128]{0,2,1:T(8,128)} fusion(bf16[128,32,289]{2,1,0:T(8,128)(2,1)S(1)} %bitcast.67, s32[128]{0:T(128)S(1)} %add_bitcast_fusion), kind=kOutput, calls=%fused_computation.3 | convolution fusion | flops 303075456 | bytes 4465152 | tf_op jit(solution)/shard_map/ps,lks->pkl/dot_general | solution.py:80
  141.2 3.0 %copy.31 = f32[128,32,128]{2,1,0:T(8,128)} copy(f32[128,32,128]{0,2,1:T(8,128)} %fusion.2) | data formatting | bytes 4194304 | tf_op jit(solution)/shard_map/ps,lks->pkl/transpose | solution.py:80
  (7 shorter events, 0.1 us)
Async XLA Ops:
  0.0 19.7 %copy-start = (f32[2,512]{1,0:T(2,128)S(1)}, f32[2,512]{1,0:T(2,128)}, u32[]{:S(2)}) copy-start(f32[2,512]{1,0:T(2,128)} %param.5) | copy-start | bytes 12292
  0.0 19.7 %copy-start.1 = (s32[512,2]{0,1:T(2,128)S(1)}, s32[512,2]{0,1:T(2,128)}, u32[]{:S(2)}) copy-start(s32[512,2]{0,1:T(2,128)} %param.6) | copy-start | bytes 12292
  6.9 23.7 %all-to-all-start = ((bf16[64,2,512]{2,1,0:T(2,128)(2,1)}), bf16[64,2,512]{2,1,0:T(2,128)(2,1)S(1)}, u32[]{:S(2)}, u32[]{:S(2)}) async-start(bf16[64,2,512]{2,1,0:T(2,128)(2,1)} %reshape.97), calls=%async_computation | async-start | bytes 262144 | tf_op jit(solution)/shard_map/all_to_all | solution.py:49
  50.4 1.0 copy-start.3
  56.7 8.0 %copy-start.2 = (s32[128,2]{0,1:T(2,128)S(1)}, s32[128,2]{0,1:T(2,128)}, u32[]{:S(2)}) copy-start(s32[128,2]{0,1:T(2,128)} %param.7) | copy-start | bytes 3076
  56.7 81.4 %all-to-all-start.1 = ((bf16[64,2,32,289]{3,2,1,0:T(8,128)(2,1)}), bf16[64,2,32,289]{3,2,1,0:T(8,128)(2,1)S(1)}, u32[]{:S(2)}, u32[]{:S(2)}) async-start(bf16[64,2,32,289]{3,2,1,0:T(8,128)(2,1)} %stack.11), calls=%async_computation.1 | async-start | bytes 6291456 | tf_op jit(solution)/shard_map/all_to_all | solution.py:69
